TPU v7x, 256 devices: a whole 4x4x8 slice. The times are simulated.
256 devices in a mesh: row: 16 (over y, x), col: 16 (over z, core).
Axes of the slice: x: 4, y: 4, z: 8, core: 2. Of those that a mesh axis runs over, the one named last changes fastest.
Arguments:
- matrix: float32 [16384, 4, 4096], P('row', None, 'col'), may hold values from -28 to 28
Outputs:
- coefficients: float32 [512, 4, 4096], P(None, None, 'col')
- remainder: float32 [16384, 4, 4096], P('row', None, 'col')
All inputs are finite; a program needn't handle non-finite values.
Results may differ from a plain program's by a relative error of at most 0.0003.
Values sent between devices are 32-bit elements; how exact they have to be, the bound alone decides.
No kernel may reach another device: no remote copies, remote signals or barrier semaphores. Data moves between devices by JAX's collectives and lax.ppermute only.
A program may use at most 64 MiB of HBM per device.

v0:
```python
import jax
import jax.numpy as jnp
from jax import lax
from jax.sharding import PartitionSpec as P

BLOCK = 256
highest = lax.Precision.HIGHEST


def spread(block, axis, holder):
    block = jnp.where(lax.axis_index(axis) == holder, block, jnp.zeros_like(block))
    return lax.psum(block, axis)


def share_panel(work, owner):
    return spread(work[:, :BLOCK], "col", owner)


def reduce_rows(partial_value):
    return lax.psum(partial_value, "row")


def project_out(work, panel):
    gram = lax.dot_general(
        panel,
        panel,
        (((0,), (0,)), ((), ())),
        precision=highest,
        preferred_element_type=jnp.float32,
    )
    lower = jnp.linalg.cholesky(reduce_rows(gram))
    factor_t = jax.scipy.linalg.solve_triangular(lower, panel.T, lower=True)
    local_terms = jnp.dot(factor_t, work, precision=highest, preferred_element_type=jnp.float32)
    coeffs = lax.psum(local_terms, "row")
    update = lax.dot_general(
        factor_t,
        coeffs,
        (((0,), (0,)), ((), ())),
        precision=highest,
        preferred_element_type=jnp.float32,
    )
    return (work - update, coeffs)


def on_device(matrix):
    row_count, block_count, width = matrix.shape
    work = matrix.reshape(row_count, block_count * width)
    pieces = []
    for owner in range(2):
        panel = share_panel(work, owner)
        work, part_coeffs = project_out(work, panel)
        pieces.append(part_coeffs)
    coeffs = jnp.concatenate(pieces, axis=0)
    coefficients = coeffs.reshape(2 * BLOCK, block_count, width)
    return (coefficients, work.reshape(row_count, block_count, width))


def solution(mesh):
    return jax.shard_map(
        on_device,
        mesh=mesh,
        in_specs=(P("row", None, "col"),),
        out_specs=(P(None, None, "col"), P("row", None, "col")),
        check_vma=False,
    )
```

profile of v0, /device:TPU:32, one launch (start us, length us, event | category | flops | bytes accessed | tf_op | source)
XLA Modules:
  0.0 806.1 jit_solution(3339477113877099299)
XLA Ops:
  7.2 5.2 copy.3
  12.4 2.3 slice_select_fusion.1
  14.8 111.5 %all-reduce.8.cloned.1.call-done = f32[1024,256]{0,1:T(8,128)} async-done(((f32[1024,256]{0,1:T(8,128)}), f32[1024,256]{0,1:T(8,128)}) %all-reduce.8.cloned.1.call-update) | async-done | bytes 1048592 | tf_op jit(solution)/shard_map/psum | solution.py:12
  126.3 3.4 fusion.24
  129.8 98.0 %all-reduce.10.cloned.1.call-done = f32[256,256]{0,1:T(8,128)} async-done(((f32[256,256]{0,1:T(8,128)}), f32[256,256]{0,1:T(8,128)}) %all-reduce.10.cloned.1.call-update) | async-done | bytes 262160 | tf_op jit(solution)/shard_map/psum | solution.py:20
  227.7 1.1 copy.5
  228.8 1.0 fusion.7
  229.8 11.7 %cholesky.130 = f32[128,128]{1,0:T(8,128)S(1)} custom-call(f32[128,128]{1,0:T(8,128)S(1)} %cholesky.194), custom_call_target="Cholesky" | custom-call | tf_op jit(solution)/shard_map/jit(cholesky)/cholesky | solution.py:31
  241.6 9.8 %custom-call.13 = f32[1,128,128]{1,2,0:T(8,128)S(1)} custom-call(f32[1,128,128]{2,1,0:T(8,128)S(1)} %get-tuple-element.49), custom_call_target="InvertDiagBlocksLowerTriangular" | custom-call | tf_op jit(solution)/shard_map/jit(cholesky)/cholesky | solution.py:31
  251.9 11.7 %cholesky.147 = f32[128,128]{1,0:T(8,128)S(1)} custom-call(f32[128,128]{1,0:T(8,128)S(1)} %convolution_subtract_fusion.5), custom_call_target="Cholesky" | custom-call | tf_op jit(solution)/shard_map/jit(cholesky)/cholesky | solution.py:31
  263.6 0.7 compare_reduce_fusion.2
  265.8 4.6 while.4
  266.3 0.6 fusion.44
  266.9 1.4 bitcast_dynamic-update-slice_fusion.4
  268.4 0.6 fusion.44
  269.0 1.4 bitcast_dynamic-update-slice_fusion.4
  270.4 19.7 %custom-call.14 = f32[2,128,128]{1,2,0:T(8,128)S(1)} custom-call(f32[2,128,128]{2,1,0:T(8,128)S(1)} %get-tuple-element.18), custom_call_target="InvertDiagBlocksLowerTriangular" | custom-call | tf_op jit(solution)/shard_map/jit(_solve_triangular)/triangular_solve | solution.py:32
  290.1 0.6 fusion.4
  291.3 0.6 fusion.13
  292.0 6.9 fusion.1
  298.9 96.7 %all-reduce.12.cloned.1.call-done = f32[256,1024]{1,0:T(8,128)} async-done(((f32[256,1024]{1,0:T(8,128)}), f32[256,1024]{1,0:T(8,128)}) %all-reduce.12.cloned.1.call-update) | async-done | bytes 1048592 | tf_op jit(solution)/shard_map/psum | solution.py:34
  395.6 7.2 convolution_subtract_fusion.1
  402.8 2.0 copy-done
  404.8 1.0 slice_select_fusion
  405.9 108.0 %all-reduce.14.cloned.1.call-done = f32[1024,256]{0,1:T(8,128)} async-done(((f32[1024,256]{0,1:T(8,128)}), f32[1024,256]{0,1:T(8,128)}) %all-reduce.14.cloned.1.call-update) | async-done | bytes 1048592 | tf_op jit(solution)/shard_map/psum | solution.py:12
  513.9 3.4 fusion.25
  517.5 97.6 %all-reduce.16.cloned.1.call-done = f32[256,256]{0,1:T(8,128)} async-done(((f32[256,256]{0,1:T(8,128)}), f32[256,256]{0,1:T(8,128)}) %all-reduce.16.cloned.1.call-update) | async-done | bytes 262160 | tf_op jit(solution)/shard_map/psum | solution.py:20
  615.1 1.1 copy.7
  616.2 1.0 fusion.6
  617.2 11.7 %cholesky.164 = f32[128,128]{1,0:T(8,128)S(1)} custom-call(f32[128,128]{1,0:T(8,128)S(1)} %cholesky.197), custom_call_target="Cholesky" | custom-call | tf_op jit(solution)/shard_map/jit(cholesky)/cholesky | solution.py:31
  629.0 9.8 %custom-call.15 = f32[1,128,128]{1,2,0:T(8,128)S(1)} custom-call(f32[1,128,128]{2,1,0:T(8,128)S(1)} %get-tuple-element.45), custom_call_target="InvertDiagBlocksLowerTriangular" | custom-call | tf_op jit(solution)/shard_map/jit(cholesky)/cholesky | solution.py:31
  639.3 11.7 %cholesky.181 = f32[128,128]{1,0:T(8,128)S(1)} custom-call(f32[128,128]{1,0:T(8,128)S(1)} %convolution_subtract_fusion.4), custom_call_target="Cholesky" | custom-call | tf_op jit(solution)/shard_map/jit(cholesky)/cholesky | solution.py:31
  651.0 0.7 compare_reduce_fusion
  651.7 0.6 compare_reduce_fusion.1
  653.8 4.3 while.5
  654.0 0.6 fusion.45
  654.6 1.4 bitcast_dynamic-update-slice_fusion.5
  656.1 0.6 fusion.45
  656.7 1.4 bitcast_dynamic-update-slice_fusion.5
  658.1 19.7 %custom-call.16 = f32[2,128,128]{1,2,0:T(8,128)S(1)} custom-call(f32[2,128,128]{2,1,0:T(8,128)S(1)} %get-tuple-element.19), custom_call_target="InvertDiagBlocksLowerTriangular" | custom-call | tf_op jit(solution)/shard_map/jit(_solve_triangular)/triangular_solve | solution.py:32
  677.8 0.6 fusion.2
  679.0 0.6 fusion.9
  679.7 6.9 fusion
  686.5 96.8 %all-reduce.18.cloned.1.call-done = f32[256,1024]{1,0:T(8,128)} async-done(((f32[256,1024]{1,0:T(8,128)}), f32[256,1024]{1,0:T(8,128)}) %all-reduce.18.cloned.1.call-update) | async-done | bytes 1048592 | tf_op jit(solution)/shard_map/psum | solution.py:34
  783.3 7.0 convolution_subtract_fusion
  790.3 5.3 copy.8
  795.6 1.4 pad_maximum_fusion
  797.0 2.0 reshape.29
  (43 shorter events, 3.0 us)
Async XLA Ops:
  7.2 119.2 %all-reduce.8.cloned.1.call-start = ((), (), s32[]{:S(2)}) async-start(), calls=%async_computation | async-start | bytes 2097152 | tf_op jit(solution)/shard_map/psum | solution.py:12
  14.8 213.0 %all-reduce.10.cloned.1.call-start = ((), (), s32[]{:S(2)}) async-start(), calls=%async_computation.1 | async-start | bytes 524288 | tf_op jit(solution)/shard_map/psum | solution.py:20
  126.3 163.8 %copy-start.1 = (f32[1024,256]{0,1:T(8,128)S(1)}, f32[1024,256]{0,1:T(8,128)}, u32[]{:S(2)}) copy-start(f32[1024,256]{0,1:T(8,128)} %all-reduce.8.cloned.1.call-done) | copy-start | bytes 3145732
  129.7 265.9 %all-reduce.12.cloned.1.call-start = ((), (), s32[]{:S(2)}) async-start(), calls=%async_computation.2 | async-start | bytes 2097152 | tf_op jit(solution)/shard_map/psum | solution.py:34
  298.8 215.0 %all-reduce.14.cloned.1.call-start = ((), (), s32[]{:S(2)}) async-start(), calls=%async_computation.3 | async-start | bytes 2097152 | tf_op jit(solution)/shard_map/psum | solution.py:12
  402.8 2.0 copy-start
  405.9 209.3 %all-reduce.16.cloned.1.call-start = ((), (), s32[]{:S(2)}) async-start(), calls=%async_computation.4 | async-start | bytes 524288 | tf_op jit(solution)/shard_map/psum | solution.py:20
  513.9 163.9 %copy-start.2 = (f32[1024,256]{0,1:T(8,128)S(1)}, f32[1024,256]{0,1:T(8,128)}, u32[]{:S(2)}) copy-start(f32[1024,256]{0,1:T(8,128)} %all-reduce.14.cloned.1.call-done) | copy-start | bytes 3145732
  517.3 266.0 %all-reduce.18.cloned.1.call-start = ((), (), s32[]{:S(2)}) async-start(), calls=%async_computation.5 | async-start | bytes 2097152 | tf_op jit(solution)/shard_map/psum | solution.py:34
  790.3 5.3 copy-start.3
Sparse Core Ops, SparseCore 0:
  14.9 111.3 all-reduce.7
  130.4 97.2 all-reduce.9
  299.0 96.5 all-reduce.11
  406.0 107.8 all-reduce.13
  517.8 97.2 all-reduce.15
  686.7 96.5 all-reduce.17
where the time goes:
time: 815 us; the launch traced here: 806 us
  waiting for transfers between devices  609 us (75%)
  other arithmetic  115 us (14%)
  matrix products  39.2 us (5%)
  local copies, waits for them, and re-layouts  25 us (3%)
  between operations  17.3 us (2%)
    psum x2, waiting for transfers between devices, spread(): return lax.psum(block, axis)  219 us
    psum x2, waiting for transfers between devices, reduce_rows(): return lax.psum(partial_value, 'row')  196 us
    psum x2, waiting for transfers between devices, project_out(): coeffs = lax.psum(local_terms, 'row')  193 us
    another operation x13, other arithmetic, project_out(): lower = jnp.linalg.cholesky(reduce_rows(gram))  68.7 us
    another operation x5, other arithmetic, project_out(): factor_t = jax.scipy.linalg.solve_triangular(lower, panel.T, lower=True)  39.4 us
  transfers between devices with their start and end apart: 6, of which 6 were waited for; matrix products, arithmetic and copies ran while one was open for 0% of the time, Pallas kernels for 0%

commit v1 on v0

--- a/solution.py
+++ b/solution.py
@@ -17,7 +17,7 @@
 
 
 def reduce_rows(partial_value):
-    return lax.psum(partial_value, "row")
+    return jnp.sum(lax.all_gather(partial_value, "row"), axis=0)
 
 
 def project_out(work, panel):

time: 815 us -> 740 us (0.908)
  waiting for transfers between devices: 609 us -> 533 us
    psum x2 -> x0, waiting for transfers between devices: 196 us -> none  [reduce_rows(): return lax.psum(partial_value, 'row')]
    all_gather x0 -> x2, waiting for transfers between devices: none -> 119 us  [reduce_rows(): return jnp.sum(lax.all_gather(partial_value, 'row'), axis=0)]
where the time goes in v1:
time: 740 us; the launch traced here: 731 us
  waiting for transfers between devices  533 us (72%)
  other arithmetic  118 us (16%)
  matrix products  39.1 us (5%)
  local copies, waits for them, and re-layouts  22.9 us (3%)
  between operations  17.2 us (2%)
    psum x2, waiting for transfers between devices, spread(): return lax.psum(block, axis)  219 us
    psum x2, waiting for transfers between devices, project_out(): coeffs = lax.psum(local_terms, 'row')  194 us
    all_gather x2, waiting for transfers between devices, reduce_rows(): return jnp.sum(lax.all_gather(partial_value, 'row'), axis=0)  119 us
    another operation x13, other arithmetic, project_out(): lower = jnp.linalg.cholesky(reduce_rows(gram))  68.7 us
    another operation x5, other arithmetic, project_out(): factor_t = jax.scipy.linalg.solve_triangular(lower, panel.T, lower=True)  39.4 us
  transfers between devices with their start and end apart: 6, of which 6 were waited for; matrix products, arithmetic and copies ran while one was open for 0% of the time, Pallas kernels for 0%

profile of v1, /device:TPU:32, one launch (start us, length us, event | category | flops | bytes accessed | tf_op | source)
XLA Modules:
  0.0 731.2 jit_solution(16209530561162008839)
XLA Ops:
  7.2 5.2 copy.7
  12.4 2.3 slice_select_fusion.1
  14.8 111.5 %all-reduce.6.cloned.1.call-done = f32[1024,256]{0,1:T(8,128)} async-done(((f32[1024,256]{0,1:T(8,128)}), f32[1024,256]{0,1:T(8,128)}) %all-reduce.6.cloned.1.call-update) | async-done | bytes 1048592 | tf_op jit(solution)/shard_map/psum | solution.py:12
  126.3 3.3 fusion.24
  129.7 59.6 %all-gather.5.cloned.1.call-done = f32[4096,256]{1,0:T(8,128)} async-done(((f32[256,256]{1,0:T(8,128)}), f32[4096,256]{1,0:T(8,128)}) %all-gather.5.cloned.1.call-update) | async-done | bytes 4194320 | tf_op jit(solution)/shard_map/all_gather | solution.py:20
  189.3 2.6 reduce_sum.18
  192.1 11.7 %cholesky.130 = f32[128,128]{1,0:T(8,128)S(1)} custom-call(f32[128,128]{1,0:T(8,128)S(1)} %cholesky.194), custom_call_target="Cholesky" | custom-call | tf_op jit(solution)/shard_map/jit(cholesky)/cholesky | solution.py:31
  203.8 9.8 %custom-call.13 = f32[1,128,128]{1,2,0:T(8,128)S(1)} custom-call(f32[1,128,128]{2,1,0:T(8,128)S(1)} %get-tuple-element.51), custom_call_target="InvertDiagBlocksLowerTriangular" | custom-call | tf_op jit(solution)/shard_map/jit(cholesky)/cholesky | solution.py:31
  214.1 11.7 %cholesky.147 = f32[128,128]{1,0:T(8,128)S(1)} custom-call(f32[128,128]{1,0:T(8,128)S(1)} %convolution_subtract_fusion.5), custom_call_target="Cholesky" | custom-call | tf_op jit(solution)/shard_map/jit(cholesky)/cholesky | solution.py:31
  225.9 0.7 compare_reduce_fusion.2
  228.0 4.4 while.4
  228.5 0.6 fusion.44
  229.1 1.4 bitcast_dynamic-update-slice_fusion.4
  230.5 0.6 fusion.44
  231.1 1.4 bitcast_dynamic-update-slice_fusion.4
  232.4 19.7 %custom-call.14 = f32[2,128,128]{1,2,0:T(8,128)S(1)} custom-call(f32[2,128,128]{2,1,0:T(8,128)S(1)} %get-tuple-element.18), custom_call_target="InvertDiagBlocksLowerTriangular" | custom-call | tf_op jit(solution)/shard_map/jit(_solve_triangular)/triangular_solve | solution.py:32
  252.1 0.6 fusion.4
  252.8 0.6 convolution_subtract_fusion.3
  253.4 0.6 fusion.13
  254.0 6.9 fusion.1
  260.9 97.0 %all-reduce.8.cloned.1.call-done = f32[256,1024]{1,0:T(8,128)} async-done(((f32[256,1024]{1,0:T(8,128)}), f32[256,1024]{1,0:T(8,128)}) %all-reduce.8.cloned.1.call-update) | async-done | bytes 1048592 | tf_op jit(solution)/shard_map/psum | solution.py:34
  358.0 7.2 convolution_subtract_fusion.1
  365.2 2.0 copy-done
  367.2 1.0 slice_select_fusion
  368.3 108.0 %all-reduce.10.cloned.1.call-done = f32[1024,256]{0,1:T(8,128)} async-done(((f32[1024,256]{0,1:T(8,128)}), f32[1024,256]{0,1:T(8,128)}) %all-reduce.10.cloned.1.call-update) | async-done | bytes 1048592 | tf_op jit(solution)/shard_map/psum | solution.py:12
  476.2 3.3 fusion.25
  479.8 59.4 %all-gather.7.cloned.1.call-done = f32[4096,256]{1,0:T(8,128)} async-done(((f32[256,256]{1,0:T(8,128)}), f32[4096,256]{1,0:T(8,128)}) %all-gather.7.cloned.1.call-update) | async-done | bytes 4194320 | tf_op jit(solution)/shard_map/all_gather | solution.py:20
  539.2 2.6 reduce_sum.19
  542.0 11.7 %cholesky.164 = f32[128,128]{1,0:T(8,128)S(1)} custom-call(f32[128,128]{1,0:T(8,128)S(1)} %cholesky.197), custom_call_target="Cholesky" | custom-call | tf_op jit(solution)/shard_map/jit(cholesky)/cholesky | solution.py:31
  553.8 9.8 %custom-call.15 = f32[1,128,128]{1,2,0:T(8,128)S(1)} custom-call(f32[1,128,128]{2,1,0:T(8,128)S(1)} %get-tuple-element.47), custom_call_target="InvertDiagBlocksLowerTriangular" | custom-call | tf_op jit(solution)/shard_map/jit(cholesky)/cholesky | solution.py:31
  564.1 11.7 %cholesky.181 = f32[128,128]{1,0:T(8,128)S(1)} custom-call(f32[128,128]{1,0:T(8,128)S(1)} %convolution_subtract_fusion.4), custom_call_target="Cholesky" | custom-call | tf_op jit(solution)/shard_map/jit(cholesky)/cholesky | solution.py:31
  575.8 0.7 compare_reduce_fusion
  576.5 0.6 compare_reduce_fusion.1
  578.6 4.3 while.5
  578.8 0.6 fusion.45
  579.4 1.4 bitcast_dynamic-update-slice_fusion.5
  580.9 0.6 fusion.45
  581.5 1.4 bitcast_dynamic-update-slice_fusion.5
  582.9 19.7 %custom-call.16 = f32[2,128,128]{1,2,0:T(8,128)S(1)} custom-call(f32[2,128,128]{2,1,0:T(8,128)S(1)} %get-tuple-element.19), custom_call_target="InvertDiagBlocksLowerTriangular" | custom-call | tf_op jit(solution)/shard_map/jit(_solve_triangular)/triangular_solve | solution.py:32
  602.6 0.6 fusion.2
  603.2 0.6 convolution_subtract_fusion.2
  603.8 0.6 fusion.9
  604.5 6.9 fusion
  611.3 97.1 %all-reduce.12.cloned.1.call-done = f32[256,1024]{1,0:T(8,128)} async-done(((f32[256,1024]{1,0:T(8,128)}), f32[256,1024]{1,0:T(8,128)}) %all-reduce.12.cloned.1.call-update) | async-done | bytes 1048592 | tf_op jit(solution)/shard_map/psum | solution.py:34
  708.4 7.0 convolution_subtract_fusion
  715.4 5.3 copy.10
  720.7 1.4 pad_maximum_fusion
  722.1 2.0 reshape.29
  (45 shorter events, 2.2 us)
Async XLA Ops:
  7.2 119.2 %all-reduce.6.cloned.1.call-start = ((), (), s32[]{:S(2)}) async-start(), calls=%async_computation | async-start | bytes 2097152 | tf_op jit(solution)/shard_map/psum | solution.py:12
  14.8 174.5 %all-gather.5.cloned.1.call-start = ((), (), s32[]{:S(2)}) async-start(), calls=%async_computation.4 | async-start | bytes 4456448 | tf_op jit(solution)/shard_map/all_gather | solution.py:20
  129.6 228.3 %all-reduce.8.cloned.1.call-start = ((), (), s32[]{:S(2)}) async-start(), calls=%async_computation.1 | async-start | bytes 2097152 | tf_op jit(solution)/shard_map/psum | solution.py:34
  189.3 62.8 %copy-start.1 = (f32[1024,256]{0,1:T(8,128)S(1)}, f32[1024,256]{0,1:T(8,128)}, u32[]{:S(2)}) copy-start(f32[1024,256]{0,1:T(8,128)} %all-reduce.6.cloned.1.call-done) | copy-start | bytes 3145732
  260.9 215.4 %all-reduce.10.cloned.1.call-start = ((), (), s32[]{:S(2)}) async-start(), calls=%async_computation.2 | async-start | bytes 2097152 | tf_op jit(solution)/shard_map/psum | solution.py:12
  365.1 2.0 copy-start
  368.2 171.0 %all-gather.7.cloned.1.call-start = ((), (), s32[]{:S(2)}) async-start(), calls=%async_computation.5 | async-start | bytes 4456448 | tf_op jit(solution)/shard_map/all_gather | solution.py:20
  479.6 228.8 %all-reduce.12.cloned.1.call-start = ((), (), s32[]{:S(2)}) async-start(), calls=%async_computation.3 | async-start | bytes 2097152 | tf_op jit(solution)/shard_map/psum | solution.py:34
  539.2 63.3 %copy-start.2 = (f32[1024,256]{0,1:T(8,128)S(1)}, f32[1024,256]{0,1:T(8,128)}, u32[]{:S(2)}) copy-start(f32[1024,256]{0,1:T(8,128)} %all-reduce.10.cloned.1.call-done) | copy-start | bytes 3145732
  715.4 5.3 copy-start.3
Sparse Core Ops, SparseCore 0:
  14.9 111.3 all-reduce.5
  129.8 59.4 all-gather.4
  261.0 96.9 all-reduce.7
  368.4 107.8 all-reduce.9
  479.7 59.4 all-gather.6
  611.5 96.9 all-reduce.11
